TPU v7x, 128 devices: a whole 4x4x4 slice. The times are simulated.
128 devices in a mesh: section: 2 (over core), seq: 16 (over z, y), head: 4 (over x).
Axes of the slice: x: 4, y: 4, z: 4, core: 2. Of those that a mesh axis runs over, the one named last changes fastest.
Arguments:
- query_vectors: bfloat16 [2, 2048, 8192], P('section', 'seq', 'head'), may hold values from -400 to 400
- key_vectors: bfloat16 [2, 2048, 8192], P('section', 'seq', 'head'), may hold values from -6 to 6
- value_vectors: bfloat16 [2, 2048, 8192], P('section', 'seq', 'head'), may hold values from -6 to 6
- prior_state: float32 [2, 64, 128, 128], P('section', 'head'), may hold values from -128 to 128
- doc_ids: int32 [2, 2048], P('section', 'seq'), may hold values from 0 to 3, never falling along the last dimension, each value on 1 to 1024 neighbouring positions
- norm_gain: float32 [2, 8192], P('section', 'head'), may hold values from 0.25 to 1.75
- residual: bfloat16 [2, 2048, 6144], P('section', 'head', 'seq'), may hold values from -6 to 6
- out_weight: bfloat16 [2, 8192, 6144], P('section', 'head', 'seq'), may hold values from -0.0625 to 0.0625
- enc_weight: bfloat16 [2, 6144, 32768], P('section', None, ('seq', 'head')), may hold values from -0.078125 to 0.078125
- enc_bias: float32 [2, 32768], P('section', ('seq', 'head')), may hold values from -5 to 5
Outputs:
- handoff: bfloat16 [2, 2048, 6144], P('section', 'head', 'seq')
- monitor: bfloat16 [2, 32, 32768], P('section', None, ('seq', 'head'))
Inputs may be any that keep to these rules, and one draw needn't show every extreme that they name: `doc_ids`: document numbers never fall along a section's tokens, are 0 at its first token and rise by at most 1 from one token to the next; a document has at most 1024 tokens, and one has exactly that many.
All inputs are finite; a program needn't handle non-finite values.
Results may differ from a plain program's by a relative error of at most 0.0039.
Values may be sent and summed in bfloat16 or wider, within the bound.
No kernel may reach another device: no remote copies, remote signals or barrier semaphores. Data moves between devices by JAX's collectives and lax.ppermute only.
A program may use at most 128 MiB of HBM per device.

v0:
```python
import jax
import jax.numpy as jnp
from jax import lax
from jax.sharding import PartitionSpec as P

HD = 128
POOL = 64
HDIM = 8192
epsilon = 1e-06


def entering(part, axis, combine, identity):
    place = lax.axis_index(axis)
    gathered = jax.tree.map(lambda a: lax.all_gather(a, axis), part)
    state = jax.tree.map(lambda a, e: jnp.zeros_like(a) + jnp.asarray(e, a.dtype), part, identity)

    def one(hop, state):
        return combine(
            state, jax.tree.map(lambda a: lax.dynamic_index_in_dim(a, hop, 0, False), gathered)
        )

    return lax.fori_loop(0, place, one, state)


def passed_along(x, axis, by):
    devices = lax.axis_size(axis)
    return lax.ppermute(x, axis, [(i, (i + by) % devices) for i in range(devices)])


def merge_states(first_pair, second_pair):
    first_state, first_doc = first_pair
    second_state, second_doc = second_pair
    top_doc = jnp.maximum(first_doc, second_doc)
    merged = jnp.where(first_doc == top_doc, first_state, 0.0) + jnp.where(
        second_doc == top_doc, second_state, 0.0
    )
    return (merged, top_doc)


def local(
    query_vectors,
    key_vectors,
    value_vectors,
    prior_state,
    doc_ids,
    norm_gain,
    residual,
    out_weight,
    enc_weight,
    enc_bias,
):
    highest = lax.Precision.HIGHEST
    row_count = query_vectors.shape[1]
    local_heads = query_vectors.shape[2] // HD
    queries = query_vectors[0].reshape(row_count, local_heads, HD)
    keys_block = key_vectors[0].reshape(row_count, local_heads, HD)
    values_block = value_vectors[0].reshape(row_count, local_heads, HD)
    doc_index = doc_ids[0]
    doc_float = doc_index.astype(jnp.float32)
    last_doc = doc_float[-1]
    keys_last = jnp.where(
        (doc_index == doc_index[-1])[:, None, None], keys_block, jnp.zeros_like(keys_block)
    )
    summary = jnp.einsum(
        "thd,the->hde", keys_last, values_block, preferred_element_type=jnp.float32
    )
    identity_pair = (jnp.zeros_like(summary), jnp.full((1,), -1.0, jnp.float32))
    earlier_state, earlier_last = entering(
        (summary, last_doc[None]), "seq", merge_states, identity_pair
    )
    earlier_doc = earlier_last[0]
    incoming_state, incoming_doc = merge_states(
        (prior_state[0], jnp.zeros((), jnp.float32)), (earlier_state, earlier_doc)
    )
    inter = jnp.einsum(
        "thd,hde->the", queries.astype(jnp.float32), incoming_state, precision=highest
    )
    inter = inter * (doc_float == incoming_doc).astype(jnp.float32)[:, None, None]
    scores = jnp.einsum("thd,uhd->htu", queries, keys_block, preferred_element_type=jnp.float32)
    positions = jnp.arange(row_count)
    same_doc = (positions[None, :] <= positions[:, None]) & (
        doc_index[:, None] == doc_index[None, :]
    )
    scores = jnp.where(same_doc[None, :, :], scores, 0.0)
    intra = jnp.einsum("htu,uhe->the", scores, values_block.astype(jnp.float32), precision=highest)
    attended = (inter + intra).reshape(row_count, local_heads * HD)
    total_square = lax.psum(jnp.sum(attended * attended, axis=1), "head")
    inverse_rms = lax.rsqrt(total_square / HDIM + epsilon)
    normed = (attended * inverse_rms[:, None] * norm_gain[0]).astype(jnp.bfloat16)
    projection = out_weight[0]
    partial_sums = jnp.dot(
        lax.all_gather(normed, "seq", axis=0, tiled=True),
        projection,
        preferred_element_type=jnp.float32,
    )
    own_rows = residual[0]
    encoder = enc_weight[0]
    latent_width = encoder.shape[1]
    reduced = lax.psum_scatter(partial_sums, "head", scatter_dimension=0, tiled=True)
    layer_out = (own_rows.astype(jnp.float32) + reduced).astype(jnp.bfloat16)
    features = lax.all_gather(layer_out, "head", axis=0, tiled=True)
    pre_scores = jnp.dot(
        lax.all_gather(features, "seq", axis=1, tiled=True),
        encoder,
        preferred_element_type=jnp.float32,
    )
    latent = jax.nn.relu(pre_scores + enc_bias[0])
    pooled = jnp.mean(latent.reshape(-1, POOL, latent_width), axis=1).astype(jnp.bfloat16)
    handoff, monitor = passed_along((layer_out[None], pooled[None]), "section", 1)
    return (handoff, monitor)


def solution(mesh):
    return jax.shard_map(
        local,
        mesh=mesh,
        in_specs=(
            P("section", "seq", "head"),
            P("section", "seq", "head"),
            P("section", "seq", "head"),
            P("section", "head", None, None),
            P("section", "seq"),
            P("section", "head"),
            P("section", "head", "seq"),
            P("section", "head", "seq"),
            P("section", None, ("seq", "head")),
            P("section", ("seq", "head")),
        ),
        out_specs=(P("section", "head", "seq"), P("section", None, ("seq", "head"))),
        check_vma=False,
    )
```

profile of v0, /device:TPU:1, one launch (start us, length us, event | category | flops | bytes accessed | tf_op | source)
XLA Modules:
  0.0 542.9 jit_solution(13562496052584884869)
XLA Ops:
  7.2 0.0 copy-start
  7.2 0.0 copy-start.4
  7.2 0.0 all-gather.13.cloned.1.call-start
  7.2 1.3 slice.8
  8.6 1.3 broadcast_compare_fusion
  9.9 1.3 copy.23
  11.2 1.3 copy.24
  12.5 1.5 fusion.14
  14.0 0.0 all-gather.13.cloned.1.call-update
  14.1 0.0 all-gather.7.cloned.1.call-start
  14.1 1.2 dynamic-slice
  15.4 0.7 bitcast_convert_fusion
  16.0 0.8 slice_dynamic-update-slice_fusion
  16.8 35.9 %all-reduce = f32[16]{0:T(128)S(1)} all-reduce(f32[16]{0:T(128)S(1)} %slice_dynamic-update-slice_fusion), channel_id=2, replica_groups=mesh['section'=2,'seq'=16,'head'=4] {'seq'}, use_global_device_ids=true, to_apply=%add | all-reduce | flops 16 | bytes 128
  52.8 1.1 copy.25
  53.9 0.0 copy-done.4
  53.9 0.1 fusion.23
  54.0 0.3 convolution_select_fusion
  54.3 2.2 convolution_bitcast_fusion
  56.5 72.5 %all-gather.13.cloned.1.call-done = f32[256,128,128]{2,1,0:T(8,128)} async-done(((f32[16,128,128]{2,1,0:T(8,128)}), f32[256,128,128]{2,1,0:T(8,128)}) %all-gather.13.cloned.1.call-update) | async-done | bytes 16777232 | tf_op jit(solution)/shard_map/all_gather | solution.py:14
  129.0 0.1 broadcast_in_dim.59
  129.1 0.0 copy-start.3
  129.1 3.6 multiply_reduce_fusion
  132.7 8.4 %psum.7 = f32[128]{0:T(128)S(1)} all-reduce(f32[128]{0:T(128)S(1)} %get-tuple-element.50), channel_id=1, replica_groups=mesh['section'=2,'seq'=16,'head'=4] {'head'}, use_global_device_ids=true, to_apply=%region_3.4 | all-reduce | flops 128 | bytes 1024 | tf_op jit(solution)/shard_map/psum | solution.py:87
  141.1 0.0 copy-done.3
  141.1 2.4 fusion.9
  143.5 0.0 all-gather.7.cloned.1.call-update
  143.5 0.0 copy-start.2
  143.5 0.0 reduce-scatter.2.cloned.1.call-start
  143.6 128.4 %all-gather.7.cloned.1.call-done = bf16[2048,2048]{0,1:T(8,128)(2,1)} async-done(((bf16[128,2048]{0,1:T(8,128)(2,1)}), bf16[2048,2048]{0,1:T(8,128)(2,1)}) %all-gather.7.cloned.1.call-update) | async-done | bytes 8388624 | tf_op jit(solution)/shard_map/all_gather | solution.py:92
  272.0 0.0 copy-done
  272.0 8.7 %fusion.4 = f32[2048,384]{1,0:T(8,128)} fusion(bf16[2048,2048]{0,1:T(8,128)(2,1)} %all-gather.7.cloned.1.call-done, bf16[1,2048,384]{2,1,0:T(8,128)(2,1)S(1)} %copy-done), kind=kOutput, calls=%fused_computation.6 | convolution fusion | flops 3221225472 | bytes 13107200 | tf_op jit(solution)/shard_map/dot_general | solution.py:91
  280.7 0.0 copy-start.5
  280.7 0.0 reduce-scatter.2.cloned.1.call-update
  280.7 0.0 all-gather.9.cloned.1.call-start
  280.7 38.5 %reduce-scatter.2.cloned.1.call-done = f32[512,384]{1,0:T(8,128)} async-done(((f32[2048,384]{1,0:T(8,128)}), f32[512,384]{1,0:T(8,128)}) %reduce-scatter.2.cloned.1.call-update) | async-done | bytes 786448 | tf_op jit(solution)/shard_map/reduce_scatter | solution.py:99
  319.2 0.0 copy-done.2
  319.2 1.9 fusion.12
  321.1 0.0 all-gather.9.cloned.1.call-update
  321.2 0.0 all-gather.11.cloned.1.call-start
  321.2 26.3 %all-gather.9.cloned.1.call-done = bf16[2048,384]{1,0:T(8,128)(2,1)} async-done(((bf16[512,384]{1,0:T(8,128)(2,1)}), bf16[2048,384]{1,0:T(8,128)(2,1)}) %all-gather.9.cloned.1.call-update) | async-done | bytes 1572880 | tf_op jit(solution)/shard_map/all_gather | solution.py:101
  347.5 0.0 all-gather.11.cloned.1.call-update
  347.6 0.8 collective-permute-start
  348.3 164.4 %all-gather.11.cloned.1.call-done = bf16[2048,6144]{1,0:T(8,128)(2,1)} async-done(((bf16[2048,384]{1,0:T(8,128)(2,1)}), bf16[2048,6144]{1,0:T(8,128)(2,1)}) %all-gather.11.cloned.1.call-update) | async-done | bytes 25165840 | tf_op jit(solution)/shard_map/all_gather | solution.py:103
  512.7 0.0 copy-done.5
  512.7 0.0 copy-start.1
  512.7 19.8 %bitcast_reduce_fusion = f32[32,512]{1,0:T(8,128)S(1)} fusion(bf16[2048,6144]{1,0:T(8,128)(2,1)} %all-gather.11.cloned.1.call-done, bf16[1,6144,512]{2,1,0:T(8,128)(2,1)} %param.20, f32[512]{0:T(512)S(1)} %bitcast.80), kind=kOutput, calls=%fused_computation.4 | convolution fusion | flops 12888031232 | bytes 31524864 | tf_op jit(solution)/shard_map/dot_general | solution.py:102
  532.5 1.6 collective-permute-start.1
  534.1 0.0 collective-permute-done
  534.1 0.9 collective-permute-done.1
  535.0 0.7 copy.46
  535.7 0.6 copy.47
  536.3 0.0 copy-done.1
  (5 shorter events, 0.0 us)
Async XLA Ops:
  7.2 264.8 %copy-start = (bf16[1,2048,384]{2,1,0:T(8,128)(2,1)S(1)}, bf16[1,2048,384]{2,1,0:T(8,128)(2,1)}, u32[]{:S(2)}) copy-start(bf16[1,2048,384]{2,1,0:T(8,128)(2,1)} %param.19) | copy-start | bytes 4718596
  7.2 46.7 %copy-start.4 = (s32[1,128]{1,0:T(1,128)S(1)}, s32[1,128]{1,0:T(1,128)}, u32[]{:S(2)}) copy-start(s32[1,128]{1,0:T(1,128)} %param.16) | copy-start | bytes 1540
  7.2 121.8 %all-gather.13.cloned.1.call-start = ((), (), s32[]{:S(2)}) async-start(), calls=%async_computation.5 | async-start | bytes 17825792 | tf_op jit(solution)/shard_map/all_gather | solution.py:14
  14.1 257.9 %all-gather.7.cloned.1.call-start = ((), (), s32[]{:S(2)}) async-start(), calls=%async_computation.1 | async-start | bytes 8912896 | tf_op jit(solution)/shard_map/all_gather | solution.py:92
  129.1 12.0 %copy-start.3 = (f32[1,2048]{1,0:T(1,128)S(1)}, f32[1,2048]{1,0:T(1,128)}, u32[]{:S(2)}) copy-start(f32[1,2048]{1,0:T(1,128)} %param.17) | copy-start | bytes 24580
  143.5 175.7 %copy-start.2 = (bf16[1,512,384]{2,1,0:T(8,128)(2,1)S(1)}, bf16[1,512,384]{2,1,0:T(8,128)(2,1)}, u32[]{:S(2)}) copy-start(bf16[1,512,384]{2,1,0:T(8,128)(2,1)} %param.18) | copy-start | bytes 1179652
  143.5 175.6 %reduce-scatter.2.cloned.1.call-start = ((), (), s32[]{:S(2)}) async-start(), calls=%async_computation.2 | async-start | bytes 3932160 | tf_op jit(solution)/shard_map/reduce_scatter | solution.py:99
  280.7 232.0 %copy-start.5 = (f32[1,512]{1,0:T(1,128)S(1)}, f32[1,512]{1,0:T(1,128)}, u32[]{:S(2)}) copy-start(f32[1,512]{1,0:T(1,128)} %param.21) | copy-start | bytes 6148
  280.7 66.8 %all-gather.9.cloned.1.call-start = ((), (), s32[]{:S(2)}) async-start(), calls=%async_computation.3 | async-start | bytes 1966080 | tf_op jit(solution)/shard_map/all_gather | solution.py:101
  321.2 191.5 %all-gather.11.cloned.1.call-start = ((), (), s32[]{:S(2)}) async-start(), calls=%async_computation.4 | async-start | bytes 26738688 | tf_op jit(solution)/shard_map/all_gather | solution.py:103
  347.6 186.6 %collective-permute-start = (bf16[1,512,384]{2,1,0:T(8,128)(2,1)}, bf16[1,512,384]{2,1,0:T(8,128)(2,1)S(1)}, u32[]{:S(2)}, u32[]{:S(2)}) collective-permute-start(bf16[1,512,384]{2,1,0:T(8,128)(2,1)} %bitcast.76), channel_id=1, source_target_pairs={{0,64},{64,0},{1,65},{65,1},{2,66},{66,2},{3,67},{67,3},{4,68},{68... | collective-permute-start | bytes 1179656 | tf_op jit(solution)/shard_map/ppermute | solution.py:27
  512.7 23.7 %copy-start.1 = (bf16[1,2048,384]{2,1,0:T(8,128)(2,1)S(1)}, bf16[1,2048,384]{2,1,0:T(8,128)(2,1)}, u32[]{:S(2)}) copy-start(bf16[1,2048,384]{2,1,0:T(8,128)(2,1)} %param.19) | copy-start | bytes 4718596
  532.5 2.5 collective-permute-start.1
Sparse Core Ops, SparseCore 0:
  14.2 114.7 all-gather.12
  143.7 128.2 all-gather.6
  280.8 38.3 reduce-scatter.1
  321.3 26.1 all-gather.8
  349.5 163.1 all-gather.10
where the time goes:
time: 544 us; the launch traced here: 543 us
  waiting for transfers between devices  431 us (79%)
  blocking collectives  44.3 us (8%)
  matrix products  36.1 us (7%)
  between operations  13.9 us (3%)
  local copies, waits for them, and re-layouts  8.65 us (2%)
  other arithmetic  6.43 us (1%)
    all_gather x1, waiting for transfers between devices, local(): lax.all_gather(features, 'seq', axis=1, tiled=True)  164 us
    all_gather x1, waiting for transfers between devices, local(): lax.all_gather(normed, 'seq', axis=0, tiled=True)  128 us
    all_gather x1, waiting for transfers between devices, entering(): gathered = jax.tree.map(lambda a: lax.all_gather(a, axis), part)  72.5 us
    reduce_scatter x1, waiting for transfers between devices, local(): lax.psum_scatter(partial_sums, 'head', scatter_dimension=0, tiled=True)  38.5 us
    unnamed x1, blocking collectives  35.9 us
    all_gather x1, waiting for transfers between devices, local(): features = lax.all_gather(layer_out, 'head', axis=0, tiled=True)  26.3 us
    dot_general x1, matrix products, local(): jnp.dot(lax.all_gather(features, 'seq', axis=1, tiled=True), encoder, pre...  19.8 us
  transfers between devices with their start and end apart: 7, of which 6 were waited for; matrix products, arithmetic and copies ran while one was open for 5% of the time, Pallas kernels for 0%

commit v1 on v0

--- a/solution.py
+++ b/solution.py
@@ -7,6 +7,22 @@
 POOL = 64
 HDIM = 8192
 epsilon = 1e-06
+
+
+def gather_around(x, axis, dim):
+    ways, here, turn = (lax.axis_size(axis), lax.axis_index(axis), x.shape[dim])
+    shape = [n * ways if d == dim else n for d, n in enumerate(x.shape)]
+    full = lax.dynamic_update_slice_in_dim(jnp.zeros(shape, x.dtype), x, here * turn, axis=dim)
+    going_up = going_down = x
+    for far in range(1, ways // 2 + 1):
+        going_up = lax.ppermute(going_up, axis, [(d, (d + 1) % ways) for d in range(ways)])
+        full = lax.dynamic_update_slice_in_dim(full, going_up, (here - far) % ways * turn, axis=dim)
+        if 2 * far < ways:
+            going_down = lax.ppermute(going_down, axis, [(d, (d - 1) % ways) for d in range(ways)])
+            full = lax.dynamic_update_slice_in_dim(
+                full, going_down, (here + far) % ways * turn, axis=dim
+            )
+    return full
 
 
 def entering(part, axis, combine, identity):
@@ -89,9 +105,7 @@
     normed = (attended * inverse_rms[:, None] * norm_gain[0]).astype(jnp.bfloat16)
     projection = out_weight[0]
     partial_sums = jnp.dot(
-        lax.all_gather(normed, "seq", axis=0, tiled=True),
-        projection,
-        preferred_element_type=jnp.float32,
+        gather_around(normed, "seq", 0), projection, preferred_element_type=jnp.float32
     )
     own_rows = residual[0]
     encoder = enc_weight[0]

time: 544 us -> 578 us (1.062)
  starting transfers between devices: 2.58 us -> 85.9 us
  waiting for transfers between devices: 431 us -> 359 us
  local copies, waits for them, and re-layouts: 8.65 us -> 31.2 us
    all_gather x1 -> x0, waiting for transfers between devices: 128 us -> none  [local(): lax.all_gather(normed, 'seq', axis=0, tiled=True)]
    ppermute x0 -> x15, starting transfers between devices: none -> 83.4 us  [the longest x7 79.1 us: gather_around(): lax.ppermute(going_down, axis, [(d, (d - 1) % ways) for d in range(ways)])]
    ppermute x0 -> x15, waiting for transfers between devices: none -> 52.5 us  [the longest x8 49.9 us: gather_around(): lax.ppermute(going_up, axis, [(d, (d + 1) % ways) for d in range(ways)])]
    dynamic_update_slice x0 -> x15, local copies, waits for them, and re-layouts: none -> 17.7 us  [the longest x8 9.25 us: gather_around(): lax.dynamic_update_slice_in_dim(full, going_up, (here - far) % ways * tur...]
  transfers between devices with their start and end apart: 7 -> 21, of which waited for: 6 -> 16; matrix products, arithmetic and copies ran while one was open for 5% -> 8% of each run, Pallas kernels for 0% -> 0%
where the time goes in v1:
time: 578 us; the launch traced here: 576 us
  waiting for transfers between devices  359 us (62%)
  starting transfers between devices  85.9 us (15%)
  blocking collectives  44.4 us (8%)
  matrix products  36.1 us (6%)
  local copies, waits for them, and re-layouts  31.2 us (5%)
  between operations  14.2 us (2%)
  other arithmetic  5.93 us (1%)
    all_gather x1, waiting for transfers between devices, local(): lax.all_gather(features, 'seq', axis=1, tiled=True)  164 us
    ppermute x7, starting transfers between devices, gather_around(): lax.ppermute(going_down, axis, [(d, (d - 1) % ways) for d in range(ways)])  79.1 us
    all_gather x1, waiting for transfers between devices, entering(): gathered = jax.tree.map(lambda a: lax.all_gather(a, axis), part)  71.7 us
    ppermute x8, waiting for transfers between devices, gather_around(): lax.ppermute(going_up, axis, [(d, (d + 1) % ways) for d in range(ways)])  49.9 us
    reduce_scatter x1, waiting for transfers between devices, local(): lax.psum_scatter(partial_sums, 'head', scatter_dimension=0, tiled=True)  42.5 us
    unnamed x1, blocking collectives  35.9 us
    all_gather x1, waiting for transfers between devices, local(): features = lax.all_gather(layer_out, 'head', axis=0, tiled=True)  26.4 us
    dot_general x1, matrix products, local(): jnp.dot(lax.all_gather(features, 'seq', axis=1, tiled=True), encoder, pre...  19.8 us
  transfers between devices with their start and end apart: 21, of which 16 were waited for; matrix products, arithmetic and copies ran while one was open for 8% of the time, Pallas kernels for 0%

profile of v1, /device:TPU:1, one launch (start us, length us, event | category | flops | bytes accessed | tf_op | source)
XLA Modules:
  0.0 576.3 jit_solution(9147088283656331684)
XLA Ops:
  7.2 1.3 slice.8
  8.6 1.3 broadcast_compare_fusion
  9.9 1.3 copy.23
  11.2 1.3 copy.24
  12.5 1.5 fusion.14
  14.1 1.2 dynamic-slice
  15.3 0.7 bitcast_convert_fusion
  16.0 0.8 slice_dynamic-update-slice_fusion
  16.8 35.9 %all-reduce = f32[16]{0:T(128)S(1)} all-reduce(f32[16]{0:T(128)S(1)} %slice_dynamic-update-slice_fusion), channel_id=2, replica_groups=mesh['section'=2,'seq'=16,'head'=4] {'seq'}, use_global_device_ids=true, to_apply=%add | all-reduce | flops 16 | bytes 128
  52.7 1.1 copy.25
  53.9 0.8 fusion.23
  54.7 0.3 convolution_select_fusion
  55.0 2.2 convolution_bitcast_fusion
  57.2 71.7 %all-gather.10.cloned.1.call-done = f32[256,128,128]{2,1,0:T(8,128)} async-done(((f32[16,128,128]{2,1,0:T(8,128)}), f32[256,128,128]{2,1,0:T(8,128)}) %all-gather.10.cloned.1.call-update) | async-done | bytes 16777232 | tf_op jit(solution)/shard_map/all_gather | solution.py:30
  129.1 0.5 copy-done.7
  129.6 3.6 multiply_reduce_fusion
  133.2 8.5 %psum.7 = f32[128]{0:T(128)S(1)} all-reduce(f32[128]{0:T(128)S(1)} %get-tuple-element.50), channel_id=1, replica_groups=mesh['section'=2,'seq'=16,'head'=4] {'head'}, use_global_device_ids=true, to_apply=%region_3.4 | all-reduce | flops 128 | bytes 1024 | tf_op jit(solution)/shard_map/psum | solution.py:103
  141.7 4.3 broadcast_in_dim.62
  146.1 1.2 constant_dynamic-update-slice_fusion.15
  147.2 4.2 collective-permute-start
  151.4 49.9 %collective-permute-start.1 = (bf16[128,2048]{0,1:T(8,128)(2,1)S(1)}, bf16[128,2048]{0,1:T(8,128)(2,1)S(1)}, u32[]{:S(2)}, u32[]{:S(2)}) collective-permute-start(bf16[128,2048]{0,1:T(8,128)(2,1)S(1)} %get-tuple-element.53), channel_id=1, source_target_pairs={{0,60},{4,0},{8,4},{12,8},{16,12},{20,16},{24,20},{28,24},{32,28},... | collective-permute-start | bytes 1572872 | tf_op jit(solution)/shard_map/ppermute | solution.py:21
  201.3 9.5 %collective-permute-done = bf16[128,2048]{0,1:T(8,128)(2,1)S(1)} collective-permute-done((bf16[128,2048]{0,1:T(8,128)(2,1)S(1)}, bf16[128,2048]{0,1:T(8,128)(2,1)S(1)}, u32[]{:S(2)}, u32[]{:S(2)}) %collective-permute-start) | collective-permute-done | bytes 524320 | tf_op jit(solution)/shard_map/ppermute | solution.py:18
  210.9 4.8 collective-permute-start.3
  215.7 8.6 %collective-permute-done.2 = bf16[128,2048]{0,1:T(8,128)(2,1)S(1)} collective-permute-done((bf16[128,2048]{0,1:T(8,128)(2,1)S(1)}, bf16[128,2048]{0,1:T(8,128)(2,1)S(1)}, u32[]{:S(2)}, u32[]{:S(2)}) %collective-permute-start.2) | collective-permute-done | bytes 524320 | tf_op jit(solution)/shard_map/ppermute | solution.py:18
  224.3 4.8 collective-permute-start.5
  229.1 7.8 %collective-permute-done.4 = bf16[128,2048]{0,1:T(8,128)(2,1)} collective-permute-done((bf16[128,2048]{0,1:T(8,128)(2,1)S(1)}, bf16[128,2048]{0,1:T(8,128)(2,1)}, u32[]{:S(2)}, u32[]{:S(2)}) %collective-permute-start.4) | collective-permute-done | bytes 524320 | tf_op jit(solution)/shard_map/ppermute | solution.py:18
  237.2 2.0 constant_dynamic-update-slice_fusion.14
  239.1 4.5 collective-permute-start.7
  243.6 1.9 constant_dynamic-update-slice_fusion.13
  245.5 2.9 collective-permute-done.6
  248.4 0.9 constant_dynamic-update-slice_fusion.12
  249.3 2.0 constant_dynamic-update-slice_fusion.11
  251.3 4.8 collective-permute-start.9
  256.1 1.9 constant_dynamic-update-slice_fusion.10
  258.0 1.8 collective-permute-done.8
  259.8 0.9 constant_dynamic-update-slice_fusion.9
  260.7 0.9 constant_dynamic-update-slice_fusion.8
  261.6 0.6 collective-permute-done.9
  262.2 5.2 collective-permute-start.11
  267.4 0.9 constant_dynamic-update-slice_fusion.7
  268.3 3.9 collective-permute-done.10
  272.2 0.9 constant_dynamic-update-slice_fusion.6
  273.1 0.9 constant_dynamic-update-slice_fusion.5
  274.0 0.9 collective-permute-done.11
  274.9 5.2 collective-permute-start.13
  280.1 0.9 constant_dynamic-update-slice_fusion.4
  281.0 4.7 collective-permute-done.12
  285.7 0.9 constant_dynamic-update-slice_fusion.3
  286.6 0.9 constant_dynamic-update-slice_fusion.2
  287.5 1.2 collective-permute-done.13
  288.7 0.9 constant_dynamic-update-slice_fusion.1
  289.5 10.7 %collective-permute-done.14 = bf16[128,2048]{0,1:T(8,128)(2,1)S(1)} collective-permute-done((bf16[128,2048]{0,1:T(8,128)(2,1)S(1)}, bf16[128,2048]{0,1:T(8,128)(2,1)S(1)}, u32[]{:S(2)}, u32[]{:S(2)}) %collective-permute-start.14) | collective-permute-done | bytes 524320 | tf_op jit(solution)/shard_map/ppermute | solution.py:18
  300.3 0.9 constant_dynamic-update-slice_fusion
  301.2 8.7 %fusion.4 = f32[2048,384]{1,0:T(8,128)} fusion(bf16[2048,2048]{0,1:T(8,128)(2,1)} %constant_dynamic-update-slice_fusion, bf16[1,2048,384]{2,1,0:T(8,128)(2,1)S(1)} %copy-done), kind=kOutput, calls=%fused_computation.6 | convolution fusion | flops 3221225472 | bytes 13107200 | tf_op jit(solution)/shard_map/dot_general | solution.py:107
  310.0 42.5 %reduce-scatter.2.cloned.1.call-done = f32[512,384]{1,0:T(8,128)} async-done(((f32[2048,384]{1,0:T(8,128)}), f32[512,384]{1,0:T(8,128)}) %reduce-scatter.2.cloned.1.call-update) | async-done | bytes 786448 | tf_op jit(solution)/shard_map/reduce_scatter | solution.py:113
  352.5 1.9 fusion.12
  354.5 26.4 %all-gather.6.cloned.1.call-done = bf16[2048,384]{1,0:T(8,128)(2,1)} async-done(((bf16[512,384]{1,0:T(8,128)(2,1)}), bf16[2048,384]{1,0:T(8,128)(2,1)}) %all-gather.6.cloned.1.call-update) | async-done | bytes 1572880 | tf_op jit(solution)/shard_map/all_gather | solution.py:115
  381.0 0.8 collective-permute-start.15
  381.7 164.4 %all-gather.8.cloned.1.call-done = bf16[2048,6144]{1,0:T(8,128)(2,1)} async-done(((bf16[2048,384]{1,0:T(8,128)(2,1)}), bf16[2048,6144]{1,0:T(8,128)(2,1)}) %all-gather.8.cloned.1.call-update) | async-done | bytes 25165840 | tf_op jit(solution)/shard_map/all_gather | solution.py:117
  546.1 19.8 %bitcast_reduce_fusion = f32[32,512]{1,0:T(8,128)S(1)} fusion(bf16[2048,6144]{1,0:T(8,128)(2,1)} %all-gather.8.cloned.1.call-done, bf16[1,6144,512]{2,1,0:T(8,128)(2,1)} %param.20, f32[512]{0:T(512)S(1)} %bitcast.80), kind=kOutput, calls=%fused_computation.4 | convolution fusion | flops 12888031232 | bytes 31524864 | tf_op jit(solution)/shard_map/dot_general | solution.py:116
  565.9 1.6 collective-permute-start.16
  567.6 0.9 collective-permute-done.16
  568.4 0.7 copy.62
  569.2 0.6 copy.63
  (43 shorter events, 0.4 us)
Async XLA Ops:
  7.2 294.0 %copy-start = (bf16[1,2048,384]{2,1,0:T(8,128)(2,1)S(1)}, bf16[1,2048,384]{2,1,0:T(8,128)(2,1)}, u32[]{:S(2)}) copy-start(bf16[1,2048,384]{2,1,0:T(8,128)(2,1)} %param.19) | copy-start | bytes 4718596
  7.2 121.7 %all-gather.10.cloned.1.call-start = ((), (), s32[]{:S(2)}) async-start(), calls=%async_computation.4 | async-start | bytes 17825792 | tf_op jit(solution)/shard_map/all_gather | solution.py:30
  14.0 338.5 %reduce-scatter.2.cloned.1.call-start = ((), (), s32[]{:S(2)}) async-start(), calls=%async_computation.1 | async-start | bytes 3932160 | tf_op jit(solution)/shard_map/reduce_scatter | solution.py:113
  128.9 0.7 copy-start.7
  129.0 17.0 %copy-start.6 = (f32[1,2048]{1,0:T(1,128)S(1)}, f32[1,2048]{1,0:T(1,128)}, u32[]{:S(2)}) copy-start(f32[1,2048]{1,0:T(1,128)} %param.17) | copy-start | bytes 24580
  133.2 12.9 %copy-start.2 = (f32[128,16,128]{0,2,1:T(8,128)S(1)}, f32[128,16,128]{0,2,1:T(8,128)}, u32[]{:S(2)}) copy-start(f32[128,16,128]{0,2,1:T(8,128)} %get-tuple-element.51) | copy-start | bytes 3145732
  147.2 63.7 %collective-permute-start = (bf16[128,2048]{0,1:T(8,128)(2,1)S(1)}, bf16[128,2048]{0,1:T(8,128)(2,1)S(1)}, u32[]{:S(2)}, u32[]{:S(2)}) collective-permute-start(bf16[128,2048]{0,1:T(8,128)(2,1)S(1)} %get-tuple-element.53), channel_id=1, source_target_pairs={{0,4},{4,8},{8,12},{12,16},{16,20},{20,24},{24,28},{28,32},{32,36}... | collective-permute-start | bytes 1572872 | tf_op jit(solution)/shard_map/ppermute | solution.py:18
  151.4 59.4 %collective-permute-start.1 = (bf16[128,2048]{0,1:T(8,128)(2,1)S(1)}, bf16[128,2048]{0,1:T(8,128)(2,1)S(1)}, u32[]{:S(2)}, u32[]{:S(2)}) collective-permute-start(bf16[128,2048]{0,1:T(8,128)(2,1)S(1)} %get-tuple-element.53), channel_id=1, source_target_pairs={{0,60},{4,0},{8,4},{12,8},{16,12},{20,16},{24,20},{28,24},{32,28},... | collective-permute-start | bytes 1572872 | tf_op jit(solution)/shard_map/ppermute | solution.py:21
  210.9 26.0 %copy-start.4 = (bf16[128,2048]{0,1:T(8,128)(2,1)}, bf16[128,2048]{0,1:T(8,128)(2,1)S(1)}, u32[]{:S(2)}) copy-start(bf16[128,2048]{0,1:T(8,128)(2,1)S(1)} %collective-permute-done) | copy-start | bytes 1572868
  210.9 13.4 %collective-permute-start.2 = (bf16[128,2048]{0,1:T(8,128)(2,1)S(1)}, bf16[128,2048]{0,1:T(8,128)(2,1)S(1)}, u32[]{:S(2)}, u32[]{:S(2)}) collective-permute-start(bf16[128,2048]{0,1:T(8,128)(2,1)S(1)} %collective-permute-done), channel_id=1, source_target_pairs={{0,4},{4,8},{8,12},{12,16},{16,20},{20,24},{24,28},{28,32},{32,36}... | collective-permute-start | bytes 1572872 | tf_op jit(solution)/shard_map/ppermute | solution.py:18
  210.9 26.0 %copy-start.3 = (bf16[128,2048]{0,1:T(8,128)(2,1)}, bf16[128,2048]{0,1:T(8,128)(2,1)S(1)}, u32[]{:S(2)}) copy-start(bf16[128,2048]{0,1:T(8,128)(2,1)S(1)} %collective-permute-done.1) | copy-start | bytes 1572868
  210.9 13.4 %collective-permute-start.3 = (bf16[128,2048]{0,1:T(8,128)(2,1)S(1)}, bf16[128,2048]{0,1:T(8,128)(2,1)}, u32[]{:S(2)}, u32[]{:S(2)}) collective-permute-start(bf16[128,2048]{0,1:T(8,128)(2,1)S(1)} %collective-permute-done.1), channel_id=1, source_target_pairs={{0,60},{4,0},{8,4},{12,8},{16,12},{20,16},{24,20},{28,24},{32,28},... | collective-permute-start | bytes 1572872 | tf_op jit(solution)/shard_map/ppermute | solution.py:21
  224.3 12.6 %collective-permute-start.4 = (bf16[128,2048]{0,1:T(8,128)(2,1)S(1)}, bf16[128,2048]{0,1:T(8,128)(2,1)}, u32[]{:S(2)}, u32[]{:S(2)}) collective-permute-start(bf16[128,2048]{0,1:T(8,128)(2,1)S(1)} %collective-permute-done.2), channel_id=1, source_target_pairs={{0,4},{4,8},{8,12},{12,16},{16,20},{20,24},{24,28},{28,32},{32,36}... | collective-permute-start | bytes 1572872 | tf_op jit(solution)/shard_map/ppermute | solution.py:18
  224.3 14.8 %collective-permute-start.5 = (bf16[128,2048]{0,1:T(8,128)(2,1)}, bf16[128,2048]{0,1:T(8,128)(2,1)S(1)}, u32[]{:S(2)}, u32[]{:S(2)}) collective-permute-start(bf16[128,2048]{0,1:T(8,128)(2,1)} %collective-permute-done.3), channel_id=1, source_target_pairs={{0,60},{4,0},{8,4},{12,8},{16,12},{20,16},{24,20},{28,24},{32,28},... | collective-permute-start | bytes 1572872 | tf_op jit(solution)/shard_map/ppermute | solution.py:21
  236.9 11.6 %collective-permute-start.6 = (bf16[128,2048]{0,1:T(8,128)(2,1)}, bf16[128,2048]{0,1:T(8,128)(2,1)S(1)}, u32[]{:S(2)}, u32[]{:S(2)}) collective-permute-start(bf16[128,2048]{0,1:T(8,128)(2,1)} %collective-permute-done.4), channel_id=1, source_target_pairs={{0,4},{4,8},{8,12},{12,16},{16,20},{20,24},{24,28},{28,32},{32,36}... | collective-permute-start | bytes 1572872 | tf_op jit(solution)/shard_map/ppermute | solution.py:18
  239.1 12.2 %collective-permute-start.7 = (bf16[128,2048]{0,1:T(8,128)(2,1)S(1)}, bf16[128,2048]{0,1:T(8,128)(2,1)S(1)}, u32[]{:S(2)}, u32[]{:S(2)}) collective-permute-start(bf16[128,2048]{0,1:T(8,128)(2,1)S(1)} %collective-permute-done.5), channel_id=1, source_target_pairs={{0,60},{4,0},{8,4},{12,8},{16,12},{20,16},{24,20},{28,24},{32,28},... | collective-permute-start | bytes 1572872 | tf_op jit(solution)/shard_map/ppermute | solution.py:21
  248.4 11.4 %collective-permute-start.8 = (bf16[128,2048]{0,1:T(8,128)(2,1)S(1)}, bf16[128,2048]{0,1:T(8,128)(2,1)S(1)}, u32[]{:S(2)}, u32[]{:S(2)}) collective-permute-start(bf16[128,2048]{0,1:T(8,128)(2,1)S(1)} %collective-permute-done.6), channel_id=1, source_target_pairs={{0,4},{4,8},{8,12},{12,16},{16,20},{20,24},{24,28},{28,32},{32,36}... | collective-permute-start | bytes 1572872 | tf_op jit(solution)/shard_map/ppermute | solution.py:18
  251.3 10.9 %collective-permute-start.9 = (bf16[128,2048]{0,1:T(8,128)(2,1)S(1)}, bf16[128,2048]{0,1:T(8,128)(2,1)S(1)}, u32[]{:S(2)}, u32[]{:S(2)}) collective-permute-start(bf16[128,2048]{0,1:T(8,128)(2,1)S(1)} %collective-permute-done.7), channel_id=1, source_target_pairs={{0,60},{4,0},{8,4},{12,8},{16,12},{20,16},{24,20},{28,24},{32,28},... | collective-permute-start | bytes 1572872 | tf_op jit(solution)/shard_map/ppermute | solution.py:21
  259.8 12.4 %collective-permute-start.10 = (bf16[128,2048]{0,1:T(8,128)(2,1)S(1)}, bf16[128,2048]{0,1:T(8,128)(2,1)S(1)}, u32[]{:S(2)}, u32[]{:S(2)}) collective-permute-start(bf16[128,2048]{0,1:T(8,128)(2,1)S(1)} %collective-permute-done.8), channel_id=1, source_target_pairs={{0,4},{4,8},{8,12},{12,16},{16,20},{20,24},{24,28},{28,32},{32,36}... | collective-permute-start | bytes 1572872 | tf_op jit(solution)/shard_map/ppermute | solution.py:18
  262.2 12.7 %collective-permute-start.11 = (bf16[128,2048]{0,1:T(8,128)(2,1)S(1)}, bf16[128,2048]{0,1:T(8,128)(2,1)S(1)}, u32[]{:S(2)}, u32[]{:S(2)}) collective-permute-start(bf16[128,2048]{0,1:T(8,128)(2,1)S(1)} %collective-permute-done.9), channel_id=1, source_target_pairs={{0,60},{4,0},{8,4},{12,8},{16,12},{20,16},{24,20},{28,24},{32,28},... | collective-permute-start | bytes 1572872 | tf_op jit(solution)/shard_map/ppermute | solution.py:21
  272.2 13.5 %collective-permute-start.12 = (bf16[128,2048]{0,1:T(8,128)(2,1)S(1)}, bf16[128,2048]{0,1:T(8,128)(2,1)S(1)}, u32[]{:S(2)}, u32[]{:S(2)}) collective-permute-start(bf16[128,2048]{0,1:T(8,128)(2,1)S(1)} %collective-permute-done.10), channel_id=1, source_target_pairs={{0,4},{4,8},{8,12},{12,16},{16,20},{20,24},{24,28},{28,32},{32,36}... | collective-permute-start | bytes 1572872 | tf_op jit(solution)/shard_map/ppermute | solution.py:18
  274.9 13.8 %collective-permute-start.13 = (bf16[128,2048]{0,1:T(8,128)(2,1)S(1)}, bf16[128,2048]{0,1:T(8,128)(2,1)S(1)}, u32[]{:S(2)}, u32[]{:S(2)}) collective-permute-start(bf16[128,2048]{0,1:T(8,128)(2,1)S(1)} %collective-permute-done.11), channel_id=1, source_target_pairs={{0,60},{4,0},{8,4},{12,8},{16,12},{20,16},{24,20},{28,24},{32,28},... | collective-permute-start | bytes 1572872 | tf_op jit(solution)/shard_map/ppermute | solution.py:21
  285.7 14.6 %collective-permute-start.14 = (bf16[128,2048]{0,1:T(8,128)(2,1)S(1)}, bf16[128,2048]{0,1:T(8,128)(2,1)S(1)}, u32[]{:S(2)}, u32[]{:S(2)}) collective-permute-start(bf16[128,2048]{0,1:T(8,128)(2,1)S(1)} %collective-permute-done.12), channel_id=1, source_target_pairs={{0,4},{4,8},{8,12},{12,16},{16,20},{20,24},{24,28},{28,32},{32,36}... | collective-permute-start | bytes 1572872 | tf_op jit(solution)/shard_map/ppermute | solution.py:18
  301.2 51.3 %copy-start.5 = (bf16[1,512,384]{2,1,0:T(8,128)(2,1)S(1)}, bf16[1,512,384]{2,1,0:T(8,128)(2,1)}, u32[]{:S(2)}) copy-start(bf16[1,512,384]{2,1,0:T(8,128)(2,1)} %param.18) | copy-start | bytes 1179652
  301.2 244.9 %copy-start.8 = (f32[1,512]{1,0:T(1,128)S(1)}, f32[1,512]{1,0:T(1,128)}, u32[]{:S(2)}) copy-start(f32[1,512]{1,0:T(1,128)} %param.21) | copy-start | bytes 6148
  309.9 71.0 %all-gather.6.cloned.1.call-start = ((), (), s32[]{:S(2)}) async-start(), calls=%async_computation.2 | async-start | bytes 1966080 | tf_op jit(solution)/shard_map/all_gather | solution.py:115
  354.5 191.6 %all-gather.8.cloned.1.call-start = ((), (), s32[]{:S(2)}) async-start(), calls=%async_computation.3 | async-start | bytes 26738688 | tf_op jit(solution)/shard_map/all_gather | solution.py:117
  381.0 186.6 %collective-permute-start.15 = (bf16[1,512,384]{2,1,0:T(8,128)(2,1)}, bf16[1,512,384]{2,1,0:T(8,128)(2,1)S(1)}, u32[]{:S(2)}, u32[]{:S(2)}) collective-permute-start(bf16[1,512,384]{2,1,0:T(8,128)(2,1)} %bitcast.76), channel_id=1, source_target_pairs={{0,64},{64,0},{1,65},{65,1},{2,66},{66,2},{3,67},{67,3},{4,68},{68... | collective-permute-start | bytes 1179656 | tf_op jit(solution)/shard_map/ppermute | solution.py:43
  546.1 23.7 %copy-start.1 = (bf16[1,2048,384]{2,1,0:T(8,128)(2,1)S(1)}, bf16[1,2048,384]{2,1,0:T(8,128)(2,1)}, u32[]{:S(2)}) copy-start(bf16[1,2048,384]{2,1,0:T(8,128)(2,1)} %param.19) | copy-start | bytes 4718596
  565.9 2.5 collective-permute-start.16
Sparse Core Ops, SparseCore 0:
  14.1 114.7 all-gather.9
  310.0 42.4 reduce-scatter.1
  354.7 26.1 all-gather.5
  382.9 163.1 all-gather.7
